TPU v7x, 256 devices: a whole 4x4x8 slice. The times are simulated.
256 devices in a mesh: det: 64 (over x, z, core), row: 4 (over y).
Axes of the slice: x: 4, y: 4, z: 8, core: 2. Of those that a mesh axis runs over, the one named last changes fastest.
Arguments:
- images: bfloat16 [384, 3, 384, 384], P('det', None, 'row'), may hold values from -6 to 6
- warp_rows: bfloat16 [384, 3, 384, 384], P('det', None, 'row'), may hold values from -0.3125 to 0.3125
- warp_cols: bfloat16 [384, 3, 384, 384], P('det'), may hold values from -0.3125 to 0.3125
- psf_coef: float32 [384, 3, 21], P('det'), may hold values from -1.25 to 1.25
- taps: float32 [21, 21], replicated, may hold values from -1.25 to 1.25
- dest_patch: int32 [3456, 1], replicated, may hold values from 0 to 63; in each aligned block of 54 rows (0 to 53, 54 to 107, ...) at most 2 rows name the same one
- dest_block: int32 [3456], replicated, may hold values from 0 to 2
- weight_index: int32 [384, 3], replicated, may hold values from 0 to 7
- weight_table: float32 [8], replicated, may hold values from 0.25 to 4
- patch_home: int32 [64], replicated, may hold values from 0 to 63, each once
Outputs:
- difference: bfloat16 [384, 3, 384, 384], P('det', None, 'row')
- coadd: bfloat16 [64, 384, 384], P('det', 'row')
Inputs may be any that keep to these rules, and one draw needn't show every extreme that they name: `dest_patch`: within the 54 rows of one device (an aligned block of rows), no patch is named more than 2 times. `patch_home`: each position once.
All inputs are finite; a program needn't handle non-finite values.
Results may differ from a plain program's by a relative error of at most 0.0082.
Values may be sent and summed in bfloat16 or wider, within the bound.
A program may use at most 128 MiB of HBM per device.

v0:
```python
import jax
import jax.numpy as jnp
from jax import lax
from jax.sharding import PartitionSpec as P

TILE = 128


def extended(value, sides, width):
    for axis, dim in sides:
        size, length = (lax.axis_size(axis), value.shape[dim])
        up = [(i, (i + 1) % size) for i in range(size - 1)]
        down = [(j, i) for i, j in up]
        last = lax.slice_in_dim(value, length - width, length, axis=dim)
        first = lax.slice_in_dim(value, 0, width, axis=dim)
        before = lax.ppermute(last, axis, up)
        after = lax.ppermute(first, axis, down)
        value = jnp.concatenate([before, value, after], axis=dim)
    return value


def toeplitz_table(values, out_len, in_len):
    span_len = values.shape[1]
    offsets = jnp.arange(in_len)[None, :] - jnp.arange(out_len)[:, None]
    picks = (offsets[:, :, None] == jnp.arange(span_len)[None, None, :]).astype(jnp.float32)
    return jnp.einsum("oij,kj->koi", picks, values.astype(jnp.float32)).astype(jnp.bfloat16)


def per_device(
    images,
    warp_rows,
    warp_cols,
    psf_coef,
    taps,
    dest_patch,
    dest_block,
    weight_index,
    weight_table,
    patch_home,
):
    det_count, visit_count, band_rows, side_cols = images.shape
    kernel_count, tap_count = taps.shape
    reach = (tap_count - 1) // 2
    tile_cols = TILE
    tile_count = side_cols // tile_cols
    det_devices = lax.axis_size("det")
    my_index = lax.axis_index("det")
    image_count = det_count * visit_count
    piece_count = image_count * tile_count
    capacity = max(2, 2 * ((piece_count + det_devices - 1) // det_devices))
    slot_count = det_devices * capacity
    padded_rows = band_rows + 2 * reach
    col_warped = jnp.einsum(
        "dvbs,dvst->dvbt", images, warp_cols, preferred_element_type=jnp.float32
    ).astype(jnp.bfloat16)
    warped = jnp.einsum(
        "dvbr,dvrs->dvbs",
        warp_rows,
        lax.all_gather(col_warped, "row", axis=2, tiled=True),
        preferred_element_type=jnp.float32,
    ).astype(jnp.bfloat16)
    padded = extended(warped, (("row", 2),), reach)
    taps_half = taps.astype(jnp.bfloat16)
    col_table = toeplitz_table(taps_half, tile_cols, tile_cols + 2 * reach)
    tiles_in = padded.reshape(image_count, padded_rows, side_cols)
    coef_rows = psf_coef.reshape(image_count, kernel_count)

    def match_image(inputs):
        tile_image, coef_row = inputs
        widened = jnp.pad(tile_image, ((0, 0), (reach, reach)))
        windows = jnp.stack(
            [
                widened[
                    :, column_tile * tile_cols : column_tile * tile_cols + tile_cols + 2 * reach
                ]
                for column_tile in range(tile_count)
            ],
            axis=1,
        )
        conv_cols = jnp.einsum(
            "rtw,kcw->krtc", windows, col_table, preferred_element_type=jnp.float32
        ).astype(jnp.bfloat16)
        conv_cols = conv_cols.reshape(kernel_count, padded_rows, side_cols)
        scaled = (coef_row[:, None] * taps).astype(jnp.bfloat16)
        row_table = toeplitz_table(scaled, band_rows, padded_rows)
        return jnp.einsum("kbr,krs->bs", row_table, conv_cols, preferred_element_type=jnp.float32)

    matched = lax.map(match_image, (tiles_in, coef_rows))
    level_count = weight_table.shape[0]
    level_onehot = (weight_index[:, :, None] == jnp.arange(level_count)[None, None, :]).astype(
        jnp.float32
    )
    weight_all = jnp.sum(level_onehot * weight_table[None, None, :], axis=2)
    weight_mine = lax.dynamic_slice_in_dim(weight_all, my_index * det_count, det_count, 0).reshape(
        image_count
    )
    weighted = (
        (weight_mine[:, None, None] * matched)
        .astype(jnp.bfloat16)
        .reshape(image_count, band_rows, tile_count, tile_cols)
    )
    patch_count = patch_home.shape[0]
    patch_ids = dest_patch[:, 0]
    owner_all = jnp.sum(
        jnp.where(patch_ids[:, None] == jnp.arange(patch_count)[None, :], patch_home[None, :], 0),
        axis=1,
    )
    owner_grid = owner_all.reshape(det_devices, piece_count)
    earlier = jnp.arange(piece_count)[None, :] < jnp.arange(piece_count)[:, None]
    rank_grid = jnp.sum(
        ((owner_grid[:, :, None] == owner_grid[:, None, :]) & earlier[None]).astype(jnp.int32),
        axis=2,
    )
    slot_grid = owner_grid * capacity + rank_grid
    slot_mine = lax.dynamic_slice_in_dim(slot_grid, my_index, 1, 0)[0]
    send_pick = (
        (jnp.arange(slot_count)[:, None] == slot_mine[None, :])
        .astype(jnp.bfloat16)
        .reshape(slot_count, image_count, tile_count)
    )
    weight_pieces = jnp.repeat(weight_all.reshape(-1), tile_count)
    to_mine = owner_all == my_index
    block_onehot = (dest_block[:, None] == jnp.arange(tile_count)[None, :]).astype(jnp.float32)
    denominator = jnp.sum(
        jnp.where(to_mine[:, None], block_onehot * weight_pieces[:, None], 0.0), axis=0
    )
    source_slot = jnp.arange(
        det_devices * piece_count
    ) // piece_count * capacity + rank_grid.reshape(-1)
    slot_onehot = (
        (source_slot[:, None] == jnp.arange(slot_count)[None, :]) & to_mine[:, None]
    ).astype(jnp.float32)
    gather_matrix = jnp.einsum("iq,is->qs", block_onehot, slot_onehot).astype(jnp.bfloat16)
    outgoing = jnp.einsum(
        "spq,pbqc->sbc", send_pick, weighted, preferred_element_type=jnp.float32
    ).astype(jnp.bfloat16)
    received = lax.all_to_all(outgoing, "det", split_axis=0, concat_axis=0, tiled=True)
    numerator = jnp.einsum(
        "qs,sbc->bqc", gather_matrix, received, preferred_element_type=jnp.float32
    )
    template = (numerator / jnp.maximum(denominator, 1.0)[None, :, None]).astype(jnp.bfloat16)
    coadd_band = template.reshape(1, band_rows, side_cols)
    returned = jnp.einsum(
        "qs,bqc->sbc", gather_matrix, template, preferred_element_type=jnp.float32
    ).astype(jnp.bfloat16)
    arrived = lax.all_to_all(returned, "det", split_axis=0, concat_axis=0, tiled=True)
    local_template = jnp.einsum(
        "spq,sbc->pbqc", send_pick, arrived, preferred_element_type=jnp.float32
    )
    difference = (
        matched.reshape(image_count, band_rows, tile_count, tile_cols) - local_template
    ).astype(jnp.bfloat16)
    difference = difference.reshape(det_count, visit_count, band_rows, side_cols)
    return (difference, coadd_band)


def solution(mesh):
    placed = (
        P("det", None, "row", None),
        P("det", None, "row", None),
        P("det", None, None, None),
        P("det", None, None),
        P(),
        P(),
        P(),
        P(),
        P(),
        P(),
    )
    return jax.shard_map(
        per_device,
        mesh=mesh,
        in_specs=placed,
        out_specs=(P("det", None, "row", None), P("det", "row", None)),
        check_vma=False,
    )
```

profile of v0, /device:TPU:1, one launch (start us, length us, event | category | flops | bytes accessed | tf_op | source)
XLA Modules:
  0.0 490.7 jit_solution(14183806398760456192)
XLA Ops:
  8.5 4.7 convolution_convert_fusion.3
  15.2 62.1 %all-gather.2.cloned.1.call-done = bf16[6,3,384,384]{3,2,1,0:T(8,128)(2,1)} async-done(((bf16[6,3,96,384]{3,2,1,0:T(8,128)(2,1)}), bf16[6,3,384,384]{3,2,1,0:T(8,128)(2,1)}) %all-gather.2.cloned.1.call-update) | async-done | bytes 5308432 | tf_op jit(solution)/shard_map/all_gather | solution.py:59
  77.3 3.6 fusion.26
  87.8 3.8 collective-permute-done.1
  93.4 198.1 %while.12 = (s32[]{:T(128)}, f32[18,96,384]{2,1,0:T(8,128)}, f32[18,21]{1,0:T(8,128)S(1)}, f32[21,21]{1,0:T(8,128)S(1)}, bf16[18,116,384]{2,1,0:T(8,128)(2,1)}, /*index=5*/bf16[21,128,148]{1,2,0:T(8,128)(2,1)}, s32[]{:T(128)}) while((s32[]{:T(128)}, f32[18,96,384]{2,1,0:T(8,128)}, f32[18,21]{1,0:T(8,128)S(1)}, f32[21,21]{1,0:T(8,128)S(1)}, ...), condition=%wide.region_1.2_spmd, body=%wide.region_0.1_spmd.sunk | while | flops 468033056 | bytes 10274817 | solution.py:88
  95.7 3.2 convert_bitcast_fusion.2
  106.7 3.2 convert_bitcast_fusion.2
  117.7 3.2 convert_bitcast_fusion.2
  128.7 3.2 convert_bitcast_fusion.2
  139.7 3.2 convert_bitcast_fusion.2
  150.7 3.2 convert_bitcast_fusion.2
  161.7 3.2 convert_bitcast_fusion.2
  172.7 3.2 convert_bitcast_fusion.2
  183.7 3.2 convert_bitcast_fusion.2
  260.7 3.2 convert_bitcast_fusion.2
  271.7 3.2 convert_bitcast_fusion.2
  294.5 3.6 reshape.134
  300.1 3.7 copy.71
  303.8 12.1 %all-to-all-start = ((bf16[128,96,128]{2,1,0:T(8,128)(2,1)}), bf16[128,96,128]{2,1,0:T(8,128)(2,1)}, u32[]{:S(2)}, u32[]{:S(2)}) async-start(bf16[128,96,128]{2,1,0:T(8,128)(2,1)} %copy.71), calls=%async_computation | async-start | bytes 6291456 | tf_op jit(solution)/shard_map/all_to_all | solution.py:137
  318.4 71.0 %all-to-all-done = bf16[128,96,128]{2,1,0:T(8,128)(2,1)} async-done(((bf16[128,96,128]{2,1,0:T(8,128)(2,1)}), bf16[128,96,128]{2,1,0:T(8,128)(2,1)}, u32[]{:S(2)}, u32[]{:S(2)}) %all-to-all-start) | async-done | bytes 3145760 | tf_op jit(solution)/shard_map/all_to_all | solution.py:137
  393.3 3.7 copy.74
  397.0 6.2 %all-to-all-start.1 = ((bf16[128,96,128]{2,1,0:T(8,128)(2,1)}), bf16[128,96,128]{2,1,0:T(8,128)(2,1)}, u32[]{:S(2)}, u32[]{:S(2)}) async-start(bf16[128,96,128]{2,1,0:T(8,128)(2,1)} %copy.74), calls=%async_computation.1 | async-start | bytes 6291456 | tf_op jit(solution)/shard_map/all_to_all | solution.py:146
  403.9 72.7 %all-to-all-done.1 = bf16[128,96,128]{2,1,0:T(8,128)(2,1)} async-done(((bf16[128,96,128]{2,1,0:T(8,128)(2,1)}), bf16[128,96,128]{2,1,0:T(8,128)(2,1)}, u32[]{:S(2)}, u32[]{:S(2)}) %all-to-all-start.1) | async-done | bytes 3145760 | tf_op jit(solution)/shard_map/all_to_all | solution.py:146
  476.7 3.3 fusion.15
  (215 shorter events, 190.0 us)
Async XLA Ops:
  7.2 1.3 copy-start
  7.2 6.1 %copy-start.9 = (f32[8]{0:T(128)S(1)}, f32[8]{0:T(128)}, u32[]{:S(2)}) copy-start(f32[8]{0:T(128)} %param.20) | copy-start | bytes 100
  7.2 6.1 %copy-start.7 = (s32[384,3]{0,1:T(4,128)S(1)}, s32[384,3]{0,1:T(4,128)}, u32[]{:S(2)}) copy-start(s32[384,3]{0,1:T(4,128)} %param.19) | copy-start | bytes 13828
  7.2 6.4 %copy-start.6 = (f32[6,3,21]{2,1,0:T(4,128)S(1)}, f32[6,3,21]{2,1,0:T(4,128)}, u32[]{:S(2)}) copy-start(f32[6,3,21]{2,1,0:T(4,128)} %param.15) | copy-start | bytes 4540
  7.2 6.4 %copy-start.5 = (s32[3456,1]{0,1:T(1,128)S(1)}, s32[3456,1]{0,1:T(1,128)}, u32[]{:S(2)}) copy-start(s32[3456,1]{0,1:T(1,128)} %param.17) | copy-start | bytes 41476
  7.2 6.5 %copy-start.8 = (s32[64]{0:T(128)S(1)}, s32[64]{0:T(128)}, u32[]{:S(2)}) copy-start(s32[64]{0:T(128)} %param.21) | copy-start | bytes 772
  7.2 70.1 %all-gather.2.cloned.1.call-start = ((), (), s32[]{:S(2)}) async-start(), calls=%async_computation.2 | async-start | bytes 6635520 | tf_op jit(solution)/shard_map/all_gather | solution.py:59
  13.2 64.1 %copy-start.2 = (bf16[6,3,96,384]{3,2,1,0:T(8,128)(2,1)S(1)}, bf16[6,3,96,384]{3,2,1,0:T(8,128)(2,1)}, u32[]{:S(2)}) copy-start(bf16[6,3,96,384]{3,2,1,0:T(8,128)(2,1)} %param.13) | copy-start | bytes 3981316
  15.2 69.8 %copy-start.3 = (f32[21,21]{1,0:T(8,128)S(1)}, f32[21,21]{1,0:T(8,128)}, u32[]{:S(2)}) copy-start(f32[21,21]{1,0:T(8,128)} %param.16) | copy-start | bytes 5296
  81.0 6.7 %collective-permute-start = (bf16[6,3,10,384]{3,2,1,0:T(8,128)(2,1)S(1)}, bf16[6,3,10,384]{3,2,1,0:T(8,128)(2,1)S(1)}, u32[]{:S(2)}, u32[]{:S(2)}) collective-permute-start(bf16[6,3,10,384]{3,2,1,0:T(8,128)(2,1)S(1)} %get-tuple-element.125), channel_id=1, source_target_pairs={{0,1},{1,2},{2,3},{4,5},{5,6},{6,7},{8,9},{9,10},{10,11},{12,13},{... | collective-permute-start | bytes 414728 | tf_op jit(solution)/shard_map/ppermute | solution.py:16
  83.7 7.9 %collective-permute-start.1 = (bf16[6,3,10,384]{3,2,1,0:T(8,128)(2,1)S(1)}, bf16[6,3,10,384]{3,2,1,0:T(8,128)(2,1)S(1)}, u32[]{:S(2)}, u32[]{:S(2)}) collective-permute-start(bf16[6,3,10,384]{3,2,1,0:T(8,128)(2,1)S(1)} %get-tuple-element.126), channel_id=1, source_target_pairs={{1,0},{2,1},{3,2},{5,4},{6,5},{7,6},{9,8},{10,9},{11,10},{13,12},{... | collective-permute-start | bytes 414728 | tf_op jit(solution)/shard_map/ppermute | solution.py:17
  303.8 13.3 %copy-start.4 = (s32[3456]{0:T(1024)S(1)}, s32[3456]{0:T(1024)}, u32[]{:S(2)}) copy-start(s32[3456]{0:T(1024)} %param.18) | copy-start | bytes 41476
  303.8 85.6 %all-to-all-start = ((bf16[128,96,128]{2,1,0:T(8,128)(2,1)}), bf16[128,96,128]{2,1,0:T(8,128)(2,1)}, u32[]{:S(2)}, u32[]{:S(2)}) async-start(bf16[128,96,128]{2,1,0:T(8,128)(2,1)} %copy.71), calls=%async_computation | async-start | bytes 6291456 | tf_op jit(solution)/shard_map/all_to_all | solution.py:137
  397.0 79.7 %all-to-all-start.1 = ((bf16[128,96,128]{2,1,0:T(8,128)(2,1)}), bf16[128,96,128]{2,1,0:T(8,128)(2,1)}, u32[]{:S(2)}, u32[]{:S(2)}) async-start(bf16[128,96,128]{2,1,0:T(8,128)(2,1)} %copy.74), calls=%async_computation.1 | async-start | bytes 6291456 | tf_op jit(solution)/shard_map/all_to_all | solution.py:146
  476.7 3.3 copy-start.1
Sparse Core Ops, SparseCore 0:
  13.4 63.8 all-gather.1
where the time goes:
time: 495 us; the launch traced here: 491 us
  waiting for transfers between devices  211 us (43%)
  matrix products  143 us (29%)
  local copies, waits for them, and re-layouts  92.9 us (19%)
  starting transfers between devices  22.4 us (5%)
  between operations  14.4 us (3%)
  other arithmetic  7.01 us (1%)
    all_to_all x1, waiting for transfers between devices, per_device(): lax.all_to_all(returned, 'det', split_axis=0, concat_axis=0, tiled=True)  72.7 us
    all_to_all x1, waiting for transfers between devices, per_device(): lax.all_to_all(outgoing, 'det', split_axis=0, concat_axis=0, tiled=True)  71 us
    all_gather x1, waiting for transfers between devices, per_device(): lax.all_gather(col_warped, 'row', axis=2, tiled=True)  62.1 us
    dot_general x18, matrix products, match_image(): jnp.einsum('rtw,kcw->krtc', windows, col_table, preferred_element_type=jn...  57.4 us
    convert_element_type x18, local copies, waits for them, and re-layouts, match_image(): conv_cols = jnp.einsum('rtw,kcw->krtc', windows, col_table, preferred_ele...  54.3 us
    dot_general x18, matrix products, match_image(): jnp.einsum('kbr,krs->bs', row_table, conv_cols, preferred_element_type=jn...  44.7 us
    dot_general x19, matrix products, toeplitz_table(): jnp.einsum('oij,kj->koi', picks, values.astype(jnp.float32))  22.1 us
    dynamic_slice x36, local copies, waits for them, and re-layouts, per_device(): matched = lax.map(match_image, (tiles_in, coef_rows))  18.7 us
  transfers between devices with their start and end apart: 5, of which 5 were waited for; matrix products, arithmetic and copies ran while one was open for 1% of the time, Pallas kernels for 0%

commit v1 on v0

--- a/solution.py
+++ b/solution.py
@@ -2,8 +2,31 @@
 import jax.numpy as jnp
 from jax import lax
 from jax.sharding import PartitionSpec as P
+from jax.lax import axis_index, axis_size, ppermute
 
 TILE = 128
+
+
+def stops_all_run(view):
+    tile_out, new, lower = (axis_size("row"), axis_index("row"), view.shape[2])
+    panels = [m * tile_out if to_i == 2 else m for to_i, m in enumerate(view.shape)]
+    oldest = lax.dynamic_update_slice_in_dim(
+        jnp.zeros(panels, view.dtype), view, new * lower, axis=2
+    )
+    reply = tall = view
+    for dev_i in range(1, tile_out // 2 + 1):
+        reply = ppermute(reply, "row", [(to_i, (to_i + 1) % tile_out) for to_i in range(tile_out)])
+        oldest = lax.dynamic_update_slice_in_dim(
+            oldest, reply, (new - dev_i) % tile_out * lower, axis=2
+        )
+        if 2 * dev_i < tile_out:
+            tall = ppermute(
+                tall, "row", [(to_i, (to_i - 1) % tile_out) for to_i in range(tile_out)]
+            )
+            oldest = lax.dynamic_update_slice_in_dim(
+                oldest, tall, (new + dev_i) % tile_out * lower, axis=2
+            )
+    return oldest
 
 
 def extended(value, sides, width):
@@ -54,10 +77,7 @@
         "dvbs,dvst->dvbt", images, warp_cols, preferred_element_type=jnp.float32
     ).astype(jnp.bfloat16)
     warped = jnp.einsum(
-        "dvbr,dvrs->dvbs",
-        warp_rows,
-        lax.all_gather(col_warped, "row", axis=2, tiled=True),
-        preferred_element_type=jnp.float32,
+        "dvbr,dvrs->dvbs", warp_rows, stops_all_run(col_warped), preferred_element_type=jnp.float32
     ).astype(jnp.bfloat16)
     padded = extended(warped, (("row", 2),), reach)
     taps_half = taps.astype(jnp.bfloat16)

time: 495 us -> 451 us (0.911)
  matrix products: 143 us -> 106 us
  waiting for transfers between devices: 211 us -> 196 us
  between operations: 14.4 us -> 0.91 us
  local copies, waits for them, and re-layouts: 92.9 us -> 104 us
  starting transfers between devices: 22.4 us -> 31.9 us
    all_gather x1 -> x0, waiting for transfers between devices: 62.1 us -> none  [per_device(): lax.all_gather(col_warped, 'row', axis=2, tiled=True)]
    ppermute x0 -> x3, waiting for transfers between devices: none -> 47.6 us  [the longest x2 47.6 us: stops_all_run(): ppermute(reply, 'row', [(to_i, (to_i + 1) % tile_out) for to_i in range(t...]
    dot_general x18, matrix products: 44.7 us -> 25.3 us  [match_image(): jnp.einsum('kbr,krs->bs', row_table, conv_cols, preferred_element_type=jn...]
    dot_general x19, matrix products: 22.1 us -> 7.16 us  [toeplitz_table(): jnp.einsum('oij,kj->koi', picks, values.astype(jnp.float32))]
    dynamic_update_slice x0 -> x3, local copies, waits for them, and re-layouts: none -> 7.75 us  [the longest x2 5.11 us: stops_all_run(): lax.dynamic_update_slice_in_dim(oldest, reply, (new - dev_i) % tile_out *...]
    ppermute x0 -> x3, starting transfers between devices: none -> 5.22 us  [the longest x2 3.66 us: stops_all_run(): ppermute(reply, 'row', [(to_i, (to_i + 1) % tile_out) for to_i in range(t...]
  transfers between devices with their start and end apart: 5 -> 7, of which waited for: 5 -> 6; matrix products, arithmetic and copies ran while one was open for 1% -> 3% of each run, Pallas kernels for 0% -> 0%
where the time goes in v1:
time: 451 us; the launch traced here: 448 us
  waiting for transfers between devices  196 us (43%)
  matrix products  106 us (24%)
  local copies, waits for them, and re-layouts  104 us (23%)
  starting transfers between devices  31.9 us (7%)
  other arithmetic  7.94 us (2%)
    all_to_all x1, waiting for transfers between devices, per_device(): lax.all_to_all(returned, 'det', split_axis=0, concat_axis=0, tiled=True)  72.7 us
    all_to_all x1, waiting for transfers between devices, per_device(): lax.all_to_all(outgoing, 'det', split_axis=0, concat_axis=0, tiled=True)  71 us
    dot_general x18, matrix products, match_image(): jnp.einsum('rtw,kcw->krtc', windows, col_table, preferred_element_type=jn...  57.2 us
    convert_element_type x18, local copies, waits for them, and re-layouts, match_image(): conv_cols = jnp.einsum('rtw,kcw->krtc', windows, col_table, preferred_ele...  54.3 us
    ppermute x2, waiting for transfers between devices, stops_all_run(): ppermute(reply, 'row', [(to_i, (to_i + 1) % tile_out) for to_i in range(t...  47.6 us
    dot_general x18, matrix products, match_image(): jnp.einsum('kbr,krs->bs', row_table, conv_cols, preferred_element_type=jn...  25.3 us
    dynamic_slice x36, local copies, waits for them, and re-layouts, per_device(): matched = lax.map(match_image, (tiles_in, coef_rows))  18.5 us
    all_to_all x1, starting transfers between devices, per_device(): lax.all_to_all(outgoing, 'det', split_axis=0, concat_axis=0, tiled=True)  16.2 us
  transfers between devices with their start and end apart: 7, of which 6 were waited for; matrix products, arithmetic and copies ran while one was open for 3% of the time, Pallas kernels for 0%

profile of v1, /device:TPU:1, one launch (start us, length us, event | category | flops | bytes accessed | tf_op | source)
XLA Modules:
  0.0 447.6 jit_solution(17785696101246625873)
XLA Ops:
  0.7 3.4 broadcast_in_dim.37
  11.6 26.8 %collective-permute-done = bf16[6,3,96,384]{3,2,1,0:T(8,128)(2,1)} collective-permute-done((bf16[6,3,96,384]{3,2,1,0:T(8,128)(2,1)S(1)}, bf16[6,3,96,384]{3,2,1,0:T(8,128)(2,1)}, u32[]{:S(2)}, u32[]{:S(2)}) %collective-permute-start) | collective-permute-done | bytes 1327136 | tf_op jit(solution)/shard_map/ppermute | solution.py:18
  47.5 20.7 %collective-permute-done.2 = bf16[6,3,96,384]{3,2,1,0:T(8,128)(2,1)} collective-permute-done((bf16[6,3,96,384]{3,2,1,0:T(8,128)(2,1)}, bf16[6,3,96,384]{3,2,1,0:T(8,128)(2,1)}, u32[]{:S(2)}, u32[]{:S(2)}) %collective-permute-start.2) | collective-permute-done | bytes 1327136 | tf_op jit(solution)/shard_map/ppermute | solution.py:18
  70.8 3.7 fusion.26
  80.2 4.2 collective-permute-done.4
  87.1 164.0 %while.12 = (s32[]{:T(128)}, f32[18,96,384]{2,1,0:T(8,128)}, f32[18,21]{1,0:T(8,128)S(1)}, f32[21,21]{1,0:T(8,128)S(1)}, bf16[18,116,384]{2,1,0:T(8,128)(2,1)}, /*index=5*/bf16[21,128,148]{1,2,0:T(8,128)(2,1)}, s32[]{:T(128)}) while((s32[]{:T(128)}, f32[18,96,384]{2,1,0:T(8,128)}, f32[18,21]{1,0:T(8,128)S(1)}, f32[21,21]{1,0:T(8,128)S(1)}, ...), condition=%wide.region_1.2_spmd, body=%wide.region_0.1_spmd.sunk | while | flops 468033056 | bytes 10153205 | solution.py:108
  88.2 3.2 convert_bitcast_fusion.2
  97.3 3.2 convert_bitcast_fusion.2
  106.5 3.2 convert_bitcast_fusion.2
  115.6 3.2 convert_bitcast_fusion.2
  124.7 3.2 convert_bitcast_fusion.2
  133.8 3.2 convert_bitcast_fusion.2
  142.9 3.2 convert_bitcast_fusion.2
  152.0 3.2 convert_bitcast_fusion.2
  161.1 3.2 convert_bitcast_fusion.2
  243.1 3.2 convert_bitcast_fusion.2
  254.2 3.6 reshape.134
  259.8 3.7 copy.71
  263.5 16.2 %all-to-all-start = ((bf16[128,96,128]{2,1,0:T(8,128)(2,1)}), bf16[128,96,128]{2,1,0:T(8,128)(2,1)}, u32[]{:S(2)}, u32[]{:S(2)}) async-start(bf16[128,96,128]{2,1,0:T(8,128)(2,1)} %copy.71), calls=%async_computation | async-start | bytes 6291456 | tf_op jit(solution)/shard_map/all_to_all | solution.py:157
  282.1 71.0 %all-to-all-done = bf16[128,96,128]{2,1,0:T(8,128)(2,1)} async-done(((bf16[128,96,128]{2,1,0:T(8,128)(2,1)}), bf16[128,96,128]{2,1,0:T(8,128)(2,1)}, u32[]{:S(2)}, u32[]{:S(2)}) %all-to-all-start) | async-done | bytes 3145760 | tf_op jit(solution)/shard_map/all_to_all | solution.py:157
  357.0 3.7 copy.74
  360.8 6.3 %all-to-all-start.1 = ((bf16[128,96,128]{2,1,0:T(8,128)(2,1)}), bf16[128,96,128]{2,1,0:T(8,128)(2,1)}, u32[]{:S(2)}, u32[]{:S(2)}) async-start(bf16[128,96,128]{2,1,0:T(8,128)(2,1)} %copy.74), calls=%async_computation.1 | async-start | bytes 6291456 | tf_op jit(solution)/shard_map/all_to_all | solution.py:166
  367.7 72.7 %all-to-all-done.1 = bf16[128,96,128]{2,1,0:T(8,128)(2,1)} async-done(((bf16[128,96,128]{2,1,0:T(8,128)(2,1)}), bf16[128,96,128]{2,1,0:T(8,128)(2,1)}, u32[]{:S(2)}, u32[]{:S(2)}) %all-to-all-start.1) | async-done | bytes 3145760 | tf_op jit(solution)/shard_map/all_to_all | solution.py:166
  440.5 3.3 fusion.15
  (224 shorter events, 174.6 us)
Async XLA Ops:
  0.6 3.4 copy-start
  0.6 4.8 %copy-start.2 = (bf16[6,3,384,384]{3,2,1,0:T(8,128)(2,1)S(1)}, bf16[6,3,384,384]{3,2,1,0:T(8,128)(2,1)}, u32[]{:S(2)}) copy-start(bf16[6,3,384,384]{3,2,1,0:T(8,128)(2,1)} %param.14) | copy-start | bytes 15925252
  5.5 34.4 %copy-start.4 = (f32[21,21]{1,0:T(8,128)S(1)}, f32[21,21]{1,0:T(8,128)}, u32[]{:S(2)}) copy-start(f32[21,21]{1,0:T(8,128)} %param.16) | copy-start | bytes 5296
  7.8 33.6 %copy-start.7 = (f32[6,3,21]{2,1,0:T(4,128)S(1)}, f32[6,3,21]{2,1,0:T(4,128)}, u32[]{:S(2)}) copy-start(f32[6,3,21]{2,1,0:T(4,128)} %param.15) | copy-start | bytes 4540
  7.8 33.6 %copy-start.8 = (s32[384,3]{0,1:T(4,128)S(1)}, s32[384,3]{0,1:T(4,128)}, u32[]{:S(2)}) copy-start(s32[384,3]{0,1:T(4,128)} %param.19) | copy-start | bytes 13828
  7.8 33.6 %copy-start.10 = (f32[8]{0:T(128)S(1)}, f32[8]{0:T(128)}, u32[]{:S(2)}) copy-start(f32[8]{0:T(128)} %param.20) | copy-start | bytes 100
  7.8 34.0 %copy-start.6 = (s32[3456,1]{0,1:T(1,128)S(1)}, s32[3456,1]{0,1:T(1,128)}, u32[]{:S(2)}) copy-start(s32[3456,1]{0,1:T(1,128)} %param.17) | copy-start | bytes 41476
  7.8 34.0 %copy-start.9 = (s32[64]{0:T(128)S(1)}, s32[64]{0:T(128)}, u32[]{:S(2)}) copy-start(s32[64]{0:T(128)} %param.21) | copy-start | bytes 772
  7.9 30.5 %collective-permute-start = (bf16[6,3,96,384]{3,2,1,0:T(8,128)(2,1)S(1)}, bf16[6,3,96,384]{3,2,1,0:T(8,128)(2,1)}, u32[]{:S(2)}, u32[]{:S(2)}) collective-permute-start(bf16[6,3,96,384]{3,2,1,0:T(8,128)(2,1)S(1)} %get-tuple-element.128), channel_id=1, source_target_pairs={{0,1},{1,2},{2,3},{3,0},{4,5},{5,6},{6,7},{7,4},{8,9},{9,10},{10,1... | collective-permute-start | bytes 3981320 | tf_op jit(solution)/shard_map/ppermute | solution.py:18
  10.0 34.9 %collective-permute-start.1 = (bf16[6,3,96,384]{3,2,1,0:T(8,128)(2,1)S(1)}, bf16[6,3,96,384]{3,2,1,0:T(8,128)(2,1)}, u32[]{:S(2)}, u32[]{:S(2)}) collective-permute-start(bf16[6,3,96,384]{3,2,1,0:T(8,128)(2,1)S(1)} %get-tuple-element.128), channel_id=1, source_target_pairs={{0,3},{1,0},{2,1},{3,2},{4,7},{5,4},{6,5},{7,6},{8,11},{9,8},{10,9... | collective-permute-start | bytes 3981320 | tf_op jit(solution)/shard_map/ppermute | solution.py:23
  38.4 29.9 %collective-permute-start.2 = (bf16[6,3,96,384]{3,2,1,0:T(8,128)(2,1)}, bf16[6,3,96,384]{3,2,1,0:T(8,128)(2,1)}, u32[]{:S(2)}, u32[]{:S(2)}) collective-permute-start(bf16[6,3,96,384]{3,2,1,0:T(8,128)(2,1)} %collective-permute-done), channel_id=1, source_target_pairs={{0,1},{1,2},{2,3},{3,0},{4,5},{5,6},{6,7},{7,4},{8,9},{9,10},{10,1... | collective-permute-start | bytes 3981320 | tf_op jit(solution)/shard_map/ppermute | solution.py:18
  44.9 25.9 %copy-start.3 = (bf16[6,3,96,384]{3,2,1,0:T(8,128)(2,1)S(1)}, bf16[6,3,96,384]{3,2,1,0:T(8,128)(2,1)}, u32[]{:S(2)}) copy-start(bf16[6,3,96,384]{3,2,1,0:T(8,128)(2,1)} %param.13) | copy-start | bytes 3981316
  74.6 5.6 %collective-permute-start.3 = (bf16[6,3,10,384]{3,2,1,0:T(8,128)(2,1)S(1)}, bf16[6,3,10,384]{3,2,1,0:T(8,128)(2,1)S(1)}, u32[]{:S(2)}, u32[]{:S(2)}) collective-permute-start(bf16[6,3,10,384]{3,2,1,0:T(8,128)(2,1)S(1)} %get-tuple-element.125), channel_id=1, source_target_pairs={{0,1},{1,2},{2,3},{4,5},{5,6},{6,7},{8,9},{9,10},{10,11},{12,13},{... | collective-permute-start | bytes 414728 | tf_op jit(solution)/shard_map/ppermute | solution.py:39
  77.4 7.1 %collective-permute-start.4 = (bf16[6,3,10,384]{3,2,1,0:T(8,128)(2,1)S(1)}, bf16[6,3,10,384]{3,2,1,0:T(8,128)(2,1)}, u32[]{:S(2)}, u32[]{:S(2)}) collective-permute-start(bf16[6,3,10,384]{3,2,1,0:T(8,128)(2,1)S(1)} %get-tuple-element.126), channel_id=1, source_target_pairs={{1,0},{2,1},{3,2},{5,4},{6,5},{7,6},{9,8},{10,9},{11,10},{13,12},{... | collective-permute-start | bytes 414728 | tf_op jit(solution)/shard_map/ppermute | solution.py:40
  263.5 17.4 %copy-start.5 = (s32[3456]{0:T(1024)S(1)}, s32[3456]{0:T(1024)}, u32[]{:S(2)}) copy-start(s32[3456]{0:T(1024)} %param.18) | copy-start | bytes 41476
  263.5 89.6 %all-to-all-start = ((bf16[128,96,128]{2,1,0:T(8,128)(2,1)}), bf16[128,96,128]{2,1,0:T(8,128)(2,1)}, u32[]{:S(2)}, u32[]{:S(2)}) async-start(bf16[128,96,128]{2,1,0:T(8,128)(2,1)} %copy.71), calls=%async_computation | async-start | bytes 6291456 | tf_op jit(solution)/shard_map/all_to_all | solution.py:157
  360.8 79.7 %all-to-all-start.1 = ((bf16[128,96,128]{2,1,0:T(8,128)(2,1)}), bf16[128,96,128]{2,1,0:T(8,128)(2,1)}, u32[]{:S(2)}, u32[]{:S(2)}) async-start(bf16[128,96,128]{2,1,0:T(8,128)(2,1)} %copy.74), calls=%async_computation.1 | async-start | bytes 6291456 | tf_op jit(solution)/shard_map/all_to_all | solution.py:166
  440.5 3.3 copy-start.1
